TPU v7x, 512 devices: a whole 4x4x16 slice. The times are simulated.
512 devices in a mesh: head: 8 (over y, x_hi), seq: 16 (over z), dp: 4 (over x_lo, core).
Axes of the slice: x: 4 (x_hi: 2, x_lo: 2; x = x_hi * 2 + x_lo), y: 4, z: 16, core: 2. Of those that a mesh axis runs over, the one named last changes fastest.
Arguments:
- teacher_query: bfloat16 [4, 2048, 3072], P('dp', 'seq', 'head'), may hold values from -6 to 6
- teacher_key: bfloat16 [4, 2048, 3072], P('dp', 'seq', 'head'), may hold values from -6 to 6
- student_query: bfloat16 [4, 2048, 512], P('dp', 'seq'), may hold values from -6 to 6
- student_key: bfloat16 [4, 2048, 512], P('dp', 'seq'), may hold values from -6 to 6
- head_mix: float32 [24, 8], P('head'), may hold values from 0.02 to 0.25
Outputs:
- grad_query: float32 [4, 2048, 512], P('dp', 'seq', 'head')
- grad_key: float32 [4, 2048, 512], P('dp', 'seq', 'head')
- grad_mix: float32 [24, 8], P('head')
- head_loss: float32 [24], P('head')
All inputs are finite; a program needn't handle non-finite values.
Results may differ from a plain program's by a relative error of at most 0.0012.
Values may be sent and summed in bfloat16 or wider, within the bound.
A program may use at most 64 MiB of HBM per device.

v0:
```python
import math
import jax
import jax.numpy as jnp
from jax import lax
from jax.sharding import PartitionSpec as P

HEADS_T = 24
HD_T = 128
HEADS_S = 8
HD_S = 64


def from_behind(block, axis, distance):
    devices = range(lax.axis_size(axis))
    route = [((i - distance) % len(devices), i) for i in devices]
    return lax.ppermute(block, axis, route)


def lift_heads(head_mix, student):
    lifted = head_mix[:, 0, None, None] * student[0][None]
    for index in range(1, HEADS_S):
        lifted = lifted + head_mix[:, index, None, None] * student[index][None]
    return lifted


def block_maps(query_t, query_s, key_t, key_s, head_mix):
    row_count = query_t.shape[0]
    key_count = key_t.shape[0]
    teacher_heads = head_mix.shape[0]
    teacher = jnp.einsum(
        "rhd,khd->hrk",
        query_t.reshape(row_count, teacher_heads, HD_T),
        key_t.reshape(key_count, teacher_heads, HD_T),
        preferred_element_type=jnp.float32,
    ) * HD_T ** (-0.5)
    student = jnp.einsum(
        "rhd,khd->hrk",
        query_s.reshape(row_count, HEADS_S, HD_S),
        key_s.reshape(key_count, HEADS_S, HD_S),
        preferred_element_type=jnp.float32,
    ) * HD_S ** (-0.5)
    lifted = lift_heads(head_mix, student)
    return (teacher, student, lifted)


def absorb(stats, teacher, lifted):
    top_t, total_t, top_l, total_l = stats
    new_t = jnp.maximum(top_t, jnp.max(teacher, axis=-1))
    new_l = jnp.maximum(top_l, jnp.max(lifted, axis=-1))
    total_t = total_t * jnp.exp(top_t - new_t) + jnp.sum(
        jnp.exp(teacher - new_t[..., None]), axis=-1
    )
    total_l = total_l * jnp.exp(top_l - new_l) + jnp.sum(
        jnp.exp(lifted - new_l[..., None]), axis=-1
    )
    return (new_t, total_t, new_l, total_l)


def pair_terms(query_t, query_s, key_t, key_s, head_mix, lse_t, lse_l):
    teacher, student, lifted = block_maps(query_t, query_s, key_t, key_s, head_mix)
    prob_t = jnp.exp(teacher - lse_t[..., None])
    prob_l = jnp.exp(lifted - lse_l[..., None])
    kl_part = jnp.sum(prob_t * (teacher - lifted), axis=-1)
    excess = prob_l - prob_t
    mix_columns = []
    mixed_rows = []
    for index in range(HEADS_S):
        mix_columns.append(jnp.sum(excess * student[index][None], axis=(1, 2)))
        mixed_rows.append(jnp.sum(head_mix[:, index, None, None] * excess, axis=0))
    mix_part = jnp.stack(mix_columns, axis=1)
    mixed_grad = jnp.stack(mixed_rows, axis=0).astype(jnp.bfloat16)
    return (kl_part, mix_part, mixed_grad)


def query_side(mixed_grad, key_s):
    key_count = key_s.shape[0]
    result = jnp.einsum(
        "hrk,khd->rhd",
        mixed_grad,
        key_s.reshape(key_count, HEADS_S, HD_S),
        preferred_element_type=jnp.float32,
    )
    return result.reshape(result.shape[0], HEADS_S * HD_S)


def key_side(mixed_grad, query_s):
    row_count = query_s.shape[0]
    result = jnp.einsum(
        "hrk,rhd->khd",
        mixed_grad,
        query_s.reshape(row_count, HEADS_S, HD_S),
        preferred_element_type=jnp.float32,
    )
    return result.reshape(result.shape[0], HEADS_S * HD_S)


def body(teacher_query, teacher_key, student_query, student_key, head_mix):
    query_t = teacher_query[0]
    query_s = student_query[0]
    own_t = teacher_key[0]
    own_s = student_key[0]
    row_count = query_t.shape[0]
    teacher_heads = head_mix.shape[0]
    group_size = lax.axis_size("seq")
    position = lax.axis_index("seq")
    shards_per = math.gcd(group_size, max(1, 512 // row_count))
    block_rows = shards_per * row_count
    block_count = group_size // shards_per
    gathered = (
        lax.all_gather(teacher_key, "seq", axis=1, tiled=True),
        lax.all_gather(student_key, "seq", axis=1, tiled=True),
    )
    keys_t = gathered[0][0]
    keys_s = gathered[1][0]

    def first_pass(index, stats):
        start = index * block_rows
        key_t = lax.dynamic_slice_in_dim(keys_t, start, block_rows, 0)
        key_s = lax.dynamic_slice_in_dim(keys_s, start, block_rows, 0)
        teacher, student, lifted = block_maps(query_t, query_s, key_t, key_s, head_mix)
        return absorb(stats, teacher, lifted)

    floor_value = jnp.full((teacher_heads, row_count), -1e30, jnp.float32)
    zero_rows = jnp.zeros((teacher_heads, row_count), jnp.float32)
    stats = lax.fori_loop(
        0, block_count, first_pass, (floor_value, zero_rows, floor_value, zero_rows)
    )
    lse_t = stats[0] + jnp.log(stats[1])
    lse_l = stats[2] + jnp.log(stats[3])
    kl_sum, mix_sum, mixed_grad = pair_terms(query_t, query_s, own_t, own_s, head_mix, lse_t, lse_l)
    query_grad = query_side(mixed_grad, own_s)
    carried = key_side(mixed_grad, query_s)

    def second_pass(turn, carry):
        kl_acc, mix_acc, query_acc, moving = carry
        moving = from_behind(moving, "seq", 1)
        start = (position - turn) % group_size * row_count
        key_t = lax.dynamic_slice_in_dim(keys_t, start, row_count, 0)
        key_s = lax.dynamic_slice_in_dim(keys_s, start, row_count, 0)
        kl_part, mix_part, mixed = pair_terms(
            query_t, query_s, key_t, key_s, head_mix, lse_t, lse_l
        )
        return (
            kl_acc + kl_part,
            mix_acc + mix_part,
            query_acc + query_side(mixed, key_s),
            moving + key_side(mixed, query_s),
        )

    kl_sum, mix_sum, query_grad, carried = lax.fori_loop(
        1, group_size, second_pass, (kl_sum, mix_sum, query_grad, carried)
    )
    key_grad = from_behind(carried, "seq", 1)
    seq_len = row_count * group_size
    images = lax.axis_size("dp") * teacher_query.shape[0]
    weight = seq_len / HEADS_T
    factor = weight * HD_S ** (-0.5)
    grad_query, grad_key = (
        lax.psum_scatter((query_grad * factor)[None], "head", scatter_dimension=2, tiled=True),
        lax.psum_scatter((key_grad * factor)[None], "head", scatter_dimension=2, tiled=True),
    )
    kl_rows = jnp.sum(kl_sum - lse_t + lse_l, axis=-1)
    mix_total, loss_total = lax.psum((mix_sum, kl_rows), ("seq", "dp"))
    grad_mix = mix_total * (weight / (images * seq_len))
    head_loss = loss_total / (images * seq_len)
    return (grad_query, grad_key, grad_mix, head_loss)


def solution(mesh):
    return jax.shard_map(
        body,
        mesh=mesh,
        in_specs=(
            P("dp", "seq", "head"),
            P("dp", "seq", "head"),
            P("dp", "seq", None),
            P("dp", "seq", None),
            P("head", None),
        ),
        out_specs=(P("dp", "seq", "head"), P("dp", "seq", "head"), P("head", None), P("head")),
        check_vma=False,
    )
```

profile of v0, /device:TPU:32, one launch (start us, length us, event | category | flops | bytes accessed | tf_op | source)
XLA Modules:
  0.0 524.6 jit_solution(4273540421250965893)
XLA Ops:
  7.2 1.6 copy.146
  8.9 1.6 copy.150
  13.5 1.2 convolution_multiply_fusion.3
  15.8 73.2 %all-gather.3.cloned.1.call-done = bf16[1,2048,384]{1,2,0:T(8,128)(2,1)} async-done(((bf16[1,128,384]{1,2,0:T(8,128)(2,1)}), bf16[1,2048,384]{1,2,0:T(8,128)(2,1)}) %all-gather.3.cloned.1.call-update) | async-done | bytes 1572880 | tf_op jit(solution)/shard_map/all_gather | solution.py:110
  89.1 76.4 %all-gather.5.cloned.1.call-done = bf16[1,2048,512]{1,2,0:T(8,128)(2,1)} async-done(((bf16[1,128,512]{1,2,0:T(8,128)(2,1)}), bf16[1,2048,512]{1,2,0:T(8,128)(2,1)}) %all-gather.5.cloned.1.call-update) | async-done | bytes 2097168 | tf_op jit(solution)/shard_map/all_gather | solution.py:111
  165.4 22.7 %while.42 = (s32[]{:T(128)}, f32[3,128]{1,0:T(4,128)S(1)}, f32[3,128]{1,0:T(4,128)S(1)}, f32[3,128]{1,0:T(4,128)S(1)}, f32[3,128]{1,0:T(4,128)S(1)}, /*index=5*/...) while((s32[]{:T(128)}, f32[3,128]{1,0:T(4,128)S(1)}, ...), condition=%wide.region_5.0_spmd.clone, body=%wide.region_0.0_spmd.clone.sunk | while | flops 125243136 | bytes 19275332 | solution.py:125
  165.4 1.1 constant_dynamic-slice_fusion.11
  169.6 1.0 constant_dynamic-slice_fusion.10
  171.2 1.1 constant_dynamic-slice_fusion.11
  175.3 1.0 constant_dynamic-slice_fusion.10
  176.8 1.1 constant_dynamic-slice_fusion.11
  180.9 1.0 constant_dynamic-slice_fusion.10
  182.5 1.1 constant_dynamic-slice_fusion.11
  186.6 1.0 constant_dynamic-slice_fusion.10
  190.6 155.4 %while.41 = (s32[]{:T(128)}, f32[3,128]{1,0:T(4,128)S(1)}, f32[3,8]{0,1:T(8,128)S(1)}, f32[128,512]{0,1:T(8,128)S(1)}, f32[128,512]{0,1:T(8,128)S(1)}, /*index=5...) while((s32[]{:T(128)}, f32[3,128]{1,0:T(4,128)S(1)}, ...), condition=%wide.region_41.42_spmd, body=%wide.region_23.41_spmd.sunk | while | flops 66486288 | bytes 9580356 | solution.py:150
  190.6 2.9 collective-permute-start
  198.9 2.9 collective-permute-start
  206.4 1.4 collective-permute-done
  207.9 2.2 collective-permute-start
  214.7 4.1 collective-permute-done
  218.9 1.9 collective-permute-start
  225.4 5.6 %collective-permute-done = f32[128,512]{0,1:T(8,128)S(1)} collective-permute-done((f32[128,512]{0,1:T(8,128)S(1)}, f32[128,512]{0,1:T(8,128)S(1)}, u32[]{:S(2)}, u32[]{:S(2)}) %collective-permute-start) | collective-permute-done | bytes 262176 | tf_op jit(solution)/shard_map/while/body/eval_jaxpr/ppermute | solution.py:16
  231.0 1.9 collective-permute-start
  237.6 5.4 %collective-permute-done = f32[128,512]{0,1:T(8,128)S(1)} collective-permute-done((f32[128,512]{0,1:T(8,128)S(1)}, f32[128,512]{0,1:T(8,128)S(1)}, u32[]{:S(2)}, u32[]{:S(2)}) %collective-permute-start) | collective-permute-done | bytes 262176 | tf_op jit(solution)/shard_map/while/body/eval_jaxpr/ppermute | solution.py:16
  243.1 1.9 collective-permute-start
  249.6 4.0 collective-permute-done
  253.7 1.9 collective-permute-start
  260.2 3.2 collective-permute-done
  263.4 1.9 collective-permute-start
  270.0 2.6 collective-permute-done
  272.7 1.9 collective-permute-start
  279.2 2.9 collective-permute-done
  282.2 1.9 collective-permute-start
  288.8 2.9 collective-permute-done
  291.7 1.9 collective-permute-start
  298.3 4.1 collective-permute-done
  302.4 1.9 collective-permute-start
  309.0 5.4 %collective-permute-done = f32[128,512]{0,1:T(8,128)S(1)} collective-permute-done((f32[128,512]{0,1:T(8,128)S(1)}, f32[128,512]{0,1:T(8,128)S(1)}, u32[]{:S(2)}, u32[]{:S(2)}) %collective-permute-start) | collective-permute-done | bytes 262176 | tf_op jit(solution)/shard_map/while/body/eval_jaxpr/ppermute | solution.py:16
  314.4 1.9 collective-permute-start
  320.9 5.7 %collective-permute-done = f32[128,512]{0,1:T(8,128)S(1)} collective-permute-done((f32[128,512]{0,1:T(8,128)S(1)}, f32[128,512]{0,1:T(8,128)S(1)}, u32[]{:S(2)}, u32[]{:S(2)}) %collective-permute-start) | collective-permute-done | bytes 262176 | tf_op jit(solution)/shard_map/while/body/eval_jaxpr/ppermute | solution.py:16
  326.7 1.9 collective-permute-start
  333.3 3.2 collective-permute-done
  336.5 1.9 collective-permute-start
  343.1 2.9 collective-permute-done
  346.8 1.9 collective-permute-start.1
  348.8 7.5 %collective-permute-done.1 = f32[128,512]{0,1:T(8,128)S(1)} collective-permute-done((f32[128,512]{0,1:T(8,128)S(1)}, f32[128,512]{0,1:T(8,128)S(1)}, u32[]{:S(2)}, u32[]{:S(2)}) %collective-permute-start.1) | collective-permute-done | bytes 262176 | tf_op jit(solution)/shard_map/ppermute | solution.py:16
  357.2 100.6 %all-reduce = (f32[3,8]{1,0:T(4,128)S(1)}, f32[3]{0:T(128)S(1)}) all-reduce(f32[3,8]{1,0:T(4,128)S(1)} %copy.175, f32[3]{0:T(128)S(1)} %add_reduce_fusion), channel_id=1, replica_groups=mesh['head'=8,'seq'=16,'dp'=4] {'seq','dp'}, use_global_device_ids=true, to_apply=%region_44.45 | all-reduce | flops 27 | bytes 216 | tf_op jit(solution)/shard_map/psum | solution.py:163
  458.9 59.2 %reduce-scatter.5.cloned.1.call-done = f32[1,128,64]{1,2,0:T(8,128)} async-done(((f32[1,128,512]{1,2,0:T(8,128)}), f32[1,128,64]{1,2,0:T(8,128)}) %reduce-scatter.5.cloned.1.call-update) | async-done | bytes 32784 | tf_op jit(solution)/shard_map/reduce_scatter | solution.py:160
  (591 shorter events, 91.0 us)
Async XLA Ops:
  7.2 8.4 %copy-start.2 = (f32[3,8]{1,0:T(4,128)S(1)}, f32[3,8]{1,0:T(4,128)}, u32[]{:S(2)}) copy-start(f32[3,8]{1,0:T(4,128)} %param.13) | copy-start | bytes 292
  7.2 81.9 %all-gather.3.cloned.1.call-start = ((), (), s32[]{:S(2)}) async-start(), calls=%async_computation.2 | async-start | bytes 1671168 | tf_op jit(solution)/shard_map/all_gather | solution.py:110
  8.9 156.6 %all-gather.5.cloned.1.call-start = ((), (), s32[]{:S(2)}) async-start(), calls=%async_computation.3 | async-start | bytes 2228224 | tf_op jit(solution)/shard_map/all_gather | solution.py:111
  10.6 448.3 %reduce-scatter.3.cloned.1.call-start = ((), (), s32[]{:S(2)}) async-start(), calls=%async_computation.4 | async-start | bytes 294912 | tf_op jit(solution)/shard_map/reduce_scatter | solution.py:159
  165.4 22.8 %copy-start.1 = (bf16[1,128,384]{1,2,0:T(8,128)(2,1)S(1)}, bf16[1,128,384]{1,2,0:T(8,128)(2,1)}, u32[]{:S(2)}) copy-start(bf16[1,128,384]{1,2,0:T(8,128)(2,1)} %copy.146) | copy-start | bytes 294916
  188.2 2.1 copy-start
  190.6 8.3 %collective-permute-start = (f32[128,512]{0,1:T(8,128)S(1)}, f32[128,512]{0,1:T(8,128)S(1)}, u32[]{:S(2)}, u32[]{:S(2)}) collective-permute-start(f32[128,512]{0,1:T(8,128)S(1)} %get-tuple-element.1076), channel_id=1, source_target_pairs={{60,0},{0,4},{4,8},{8,12},{12,16},{16,20},{20,24},{24,28},{28,32},... | collective-permute-start | bytes 786440 | tf_op jit(solution)/shard_map/while/body/eval_jaxpr/ppermute | solution.py:16
  198.9 8.9 %collective-permute-start = (f32[128,512]{0,1:T(8,128)S(1)}, f32[128,512]{0,1:T(8,128)S(1)}, u32[]{:S(2)}, u32[]{:S(2)}) collective-permute-start(f32[128,512]{0,1:T(8,128)S(1)} %get-tuple-element.1076), channel_id=1, source_target_pairs={{60,0},{0,4},{4,8},{8,12},{12,16},{16,20},{20,24},{24,28},{28,32},... | collective-permute-start | bytes 786440 | tf_op jit(solution)/shard_map/while/body/eval_jaxpr/ppermute | solution.py:16
  207.9 11.0 %collective-permute-start = (f32[128,512]{0,1:T(8,128)S(1)}, f32[128,512]{0,1:T(8,128)S(1)}, u32[]{:S(2)}, u32[]{:S(2)}) collective-permute-start(f32[128,512]{0,1:T(8,128)S(1)} %get-tuple-element.1076), channel_id=1, source_target_pairs={{60,0},{0,4},{4,8},{8,12},{12,16},{16,20},{20,24},{24,28},{28,32},... | collective-permute-start | bytes 786440 | tf_op jit(solution)/shard_map/while/body/eval_jaxpr/ppermute | solution.py:16
  218.9 12.1 %collective-permute-start = (f32[128,512]{0,1:T(8,128)S(1)}, f32[128,512]{0,1:T(8,128)S(1)}, u32[]{:S(2)}, u32[]{:S(2)}) collective-permute-start(f32[128,512]{0,1:T(8,128)S(1)} %get-tuple-element.1076), channel_id=1, source_target_pairs={{60,0},{0,4},{4,8},{8,12},{12,16},{16,20},{20,24},{24,28},{28,32},... | collective-permute-start | bytes 786440 | tf_op jit(solution)/shard_map/while/body/eval_jaxpr/ppermute | solution.py:16
  231.0 12.0 %collective-permute-start = (f32[128,512]{0,1:T(8,128)S(1)}, f32[128,512]{0,1:T(8,128)S(1)}, u32[]{:S(2)}, u32[]{:S(2)}) collective-permute-start(f32[128,512]{0,1:T(8,128)S(1)} %get-tuple-element.1076), channel_id=1, source_target_pairs={{60,0},{0,4},{4,8},{8,12},{12,16},{16,20},{20,24},{24,28},{28,32},... | collective-permute-start | bytes 786440 | tf_op jit(solution)/shard_map/while/body/eval_jaxpr/ppermute | solution.py:16
  243.1 10.6 %collective-permute-start = (f32[128,512]{0,1:T(8,128)S(1)}, f32[128,512]{0,1:T(8,128)S(1)}, u32[]{:S(2)}, u32[]{:S(2)}) collective-permute-start(f32[128,512]{0,1:T(8,128)S(1)} %get-tuple-element.1076), channel_id=1, source_target_pairs={{60,0},{0,4},{4,8},{8,12},{12,16},{16,20},{20,24},{24,28},{28,32},... | collective-permute-start | bytes 786440 | tf_op jit(solution)/shard_map/while/body/eval_jaxpr/ppermute | solution.py:16
  253.7 9.7 %collective-permute-start = (f32[128,512]{0,1:T(8,128)S(1)}, f32[128,512]{0,1:T(8,128)S(1)}, u32[]{:S(2)}, u32[]{:S(2)}) collective-permute-start(f32[128,512]{0,1:T(8,128)S(1)} %get-tuple-element.1076), channel_id=1, source_target_pairs={{60,0},{0,4},{4,8},{8,12},{12,16},{16,20},{20,24},{24,28},{28,32},... | collective-permute-start | bytes 786440 | tf_op jit(solution)/shard_map/while/body/eval_jaxpr/ppermute | solution.py:16
  263.4 9.2 %collective-permute-start = (f32[128,512]{0,1:T(8,128)S(1)}, f32[128,512]{0,1:T(8,128)S(1)}, u32[]{:S(2)}, u32[]{:S(2)}) collective-permute-start(f32[128,512]{0,1:T(8,128)S(1)} %get-tuple-element.1076), channel_id=1, source_target_pairs={{60,0},{0,4},{4,8},{8,12},{12,16},{16,20},{20,24},{24,28},{28,32},... | collective-permute-start | bytes 786440 | tf_op jit(solution)/shard_map/while/body/eval_jaxpr/ppermute | solution.py:16
  272.7 9.5 %collective-permute-start = (f32[128,512]{0,1:T(8,128)S(1)}, f32[128,512]{0,1:T(8,128)S(1)}, u32[]{:S(2)}, u32[]{:S(2)}) collective-permute-start(f32[128,512]{0,1:T(8,128)S(1)} %get-tuple-element.1076), channel_id=1, source_target_pairs={{60,0},{0,4},{4,8},{8,12},{12,16},{16,20},{20,24},{24,28},{28,32},... | collective-permute-start | bytes 786440 | tf_op jit(solution)/shard_map/while/body/eval_jaxpr/ppermute | solution.py:16
  282.2 9.5 %collective-permute-start = (f32[128,512]{0,1:T(8,128)S(1)}, f32[128,512]{0,1:T(8,128)S(1)}, u32[]{:S(2)}, u32[]{:S(2)}) collective-permute-start(f32[128,512]{0,1:T(8,128)S(1)} %get-tuple-element.1076), channel_id=1, source_target_pairs={{60,0},{0,4},{4,8},{8,12},{12,16},{16,20},{20,24},{24,28},{28,32},... | collective-permute-start | bytes 786440 | tf_op jit(solution)/shard_map/while/body/eval_jaxpr/ppermute | solution.py:16
  291.7 10.7 %collective-permute-start = (f32[128,512]{0,1:T(8,128)S(1)}, f32[128,512]{0,1:T(8,128)S(1)}, u32[]{:S(2)}, u32[]{:S(2)}) collective-permute-start(f32[128,512]{0,1:T(8,128)S(1)} %get-tuple-element.1076), channel_id=1, source_target_pairs={{60,0},{0,4},{4,8},{8,12},{12,16},{16,20},{20,24},{24,28},{28,32},... | collective-permute-start | bytes 786440 | tf_op jit(solution)/shard_map/while/body/eval_jaxpr/ppermute | solution.py:16
  302.4 11.9 %collective-permute-start = (f32[128,512]{0,1:T(8,128)S(1)}, f32[128,512]{0,1:T(8,128)S(1)}, u32[]{:S(2)}, u32[]{:S(2)}) collective-permute-start(f32[128,512]{0,1:T(8,128)S(1)} %get-tuple-element.1076), channel_id=1, source_target_pairs={{60,0},{0,4},{4,8},{8,12},{12,16},{16,20},{20,24},{24,28},{28,32},... | collective-permute-start | bytes 786440 | tf_op jit(solution)/shard_map/while/body/eval_jaxpr/ppermute | solution.py:16
  314.4 12.3 %collective-permute-start = (f32[128,512]{0,1:T(8,128)S(1)}, f32[128,512]{0,1:T(8,128)S(1)}, u32[]{:S(2)}, u32[]{:S(2)}) collective-permute-start(f32[128,512]{0,1:T(8,128)S(1)} %get-tuple-element.1076), channel_id=1, source_target_pairs={{60,0},{0,4},{4,8},{8,12},{12,16},{16,20},{20,24},{24,28},{28,32},... | collective-permute-start | bytes 786440 | tf_op jit(solution)/shard_map/while/body/eval_jaxpr/ppermute | solution.py:16
  326.7 9.7 %collective-permute-start = (f32[128,512]{0,1:T(8,128)S(1)}, f32[128,512]{0,1:T(8,128)S(1)}, u32[]{:S(2)}, u32[]{:S(2)}) collective-permute-start(f32[128,512]{0,1:T(8,128)S(1)} %get-tuple-element.1076), channel_id=1, source_target_pairs={{60,0},{0,4},{4,8},{8,12},{12,16},{16,20},{20,24},{24,28},{28,32},... | collective-permute-start | bytes 786440 | tf_op jit(solution)/shard_map/while/body/eval_jaxpr/ppermute | solution.py:16
  336.5 9.5 %collective-permute-start = (f32[128,512]{0,1:T(8,128)S(1)}, f32[128,512]{0,1:T(8,128)S(1)}, u32[]{:S(2)}, u32[]{:S(2)}) collective-permute-start(f32[128,512]{0,1:T(8,128)S(1)} %get-tuple-element.1076), channel_id=1, source_target_pairs={{60,0},{0,4},{4,8},{8,12},{12,16},{16,20},{20,24},{24,28},{28,32},... | collective-permute-start | bytes 786440 | tf_op jit(solution)/shard_map/while/body/eval_jaxpr/ppermute | solution.py:16
  346.8 171.3 %reduce-scatter.5.cloned.1.call-start = ((), (), s32[]{:S(2)}) async-start(), calls=%async_computation.5 | async-start | bytes 294912 | tf_op jit(solution)/shard_map/reduce_scatter | solution.py:160
  346.8 9.5 %collective-permute-start.1 = (f32[128,512]{0,1:T(8,128)S(1)}, f32[128,512]{0,1:T(8,128)S(1)}, u32[]{:S(2)}, u32[]{:S(2)}) collective-permute-start(f32[128,512]{0,1:T(8,128)S(1)} %get-tuple-element.493), channel_id=1, source_target_pairs={{60,0},{0,4},{4,8},{8,12},{12,16},{16,20},{20,24},{24,28},{28,32},... | collective-permute-start | bytes 786440 | tf_op jit(solution)/shard_map/ppermute | solution.py:16
Sparse Core Ops, SparseCore 0:
  10.0 79.0 all-gather.2
  91.1 74.3 all-gather.4
  346.9 81.1 reduce-scatter.2
  432.9 85.1 reduce-scatter.4
where the time goes:
time: 526 us; the launch traced here: 525 us
  waiting for transfers between devices  270 us (51%)
  blocking collectives  101 us (19%)
  local copies, waits for them, and re-layouts  65.5 us (12%)
  starting transfers between devices  33.2 us (6%)
  matrix products  20.9 us (4%)
  other arithmetic  16.5 us (3%)
  between operations  14.1 us (3%)
    psum x1, blocking collectives, body(): mix_total, loss_total = lax.psum((mix_sum, kl_rows), ('seq', 'dp'))  101 us
    all_gather x1, waiting for transfers between devices, body(): lax.all_gather(student_key, 'seq', axis=1, tiled=True)  76.4 us
    all_gather x1, waiting for transfers between devices, body(): lax.all_gather(teacher_key, 'seq', axis=1, tiled=True)  73.2 us
    ppermute x16, waiting for transfers between devices, from_behind(): return lax.ppermute(block, axis, route)  61.6 us
    reduce_scatter x1, waiting for transfers between devices, body(): lax.psum_scatter((key_grad * factor)[None], 'head', scatter_dimension=2,...  59.2 us
    ppermute x16, starting transfers between devices, from_behind(): return lax.ppermute(block, axis, route)  33 us
    reduce_sum x128, local copies, waits for them, and re-layouts, pair_terms(): mixed_rows.append(jnp.sum(head_mix[:, index, None, None] * excess, axis=0))  15.2 us
    dynamic_slice x15, local copies, waits for them, and re-layouts, second_pass(): key_s = lax.dynamic_slice_in_dim(keys_s, start, row_count, 0)  13.8 us
  transfers between devices with their start and end apart: 20, of which 19 were waited for; matrix products, arithmetic and copies ran while one was open for 14% of the time, Pallas kernels for 0%

commit v1 on v0

--- a/solution.py
+++ b/solution.py
@@ -8,6 +8,24 @@
 HD_T = 128
 HEADS_S = 8
 HD_S = 64
+
+
+def collect(shard, axis, dim):
+    ways, here, step = (lax.axis_size(axis), lax.axis_index(axis), shard.shape[dim])
+    shape = [n * ways if d == dim else n for d, n in enumerate(shard.shape)]
+    full = lax.dynamic_update_slice_in_dim(
+        jnp.zeros(shape, shard.dtype), shard, here * step, axis=dim
+    )
+    going_up = going_down = shard
+    for far in range(1, ways // 2 + 1):
+        going_up = lax.ppermute(going_up, axis, [(d, (d + 1) % ways) for d in range(ways)])
+        full = lax.dynamic_update_slice_in_dim(full, going_up, (here - far) % ways * step, axis=dim)
+        if 2 * far < ways:
+            going_down = lax.ppermute(going_down, axis, [(d, (d - 1) % ways) for d in range(ways)])
+            full = lax.dynamic_update_slice_in_dim(
+                full, going_down, (here + far) % ways * step, axis=dim
+            )
+    return full
 
 
 def from_behind(block, axis, distance):
@@ -108,7 +126,7 @@
     block_count = group_size // shards_per
     gathered = (
         lax.all_gather(teacher_key, "seq", axis=1, tiled=True),
-        lax.all_gather(student_key, "seq", axis=1, tiled=True),
+        collect(student_key, "seq", 1),
     )
     keys_t = gathered[0][0]
     keys_s = gathered[1][0]

time: 526 us -> 456 us (0.87)
  waiting for transfers between devices: 270 us -> 136 us
  starting transfers between devices: 33.2 us -> 87.7 us
  local copies, waits for them, and re-layouts: 65.5 us -> 75.8 us
    all_gather x1 -> x0, waiting for transfers between devices: 76.4 us -> none  [body(): lax.all_gather(student_key, 'seq', axis=1, tiled=True)]
    all_gather x1, waiting for transfers between devices: 73.2 us -> 12.6 us  [body(): lax.all_gather(teacher_key, 'seq', axis=1, tiled=True)]
    ppermute x0 -> x15, starting transfers between devices: none -> 53.6 us  [the longest x7 36.4 us: collect(): lax.ppermute(going_down, axis, [(d, (d - 1) % ways) for d in range(ways)])]
    dynamic_update_slice x0 -> x16, local copies, waits for them, and re-layouts: none -> 10.9 us  [the longest x8 5.47 us: collect(): lax.dynamic_update_slice_in_dim(full, going_up, (here - far) % ways * ste...]
    ppermute x0 -> x15, waiting for transfers between devices: none -> 7.29 us  [the longest x8 7.22 us: collect(): lax.ppermute(going_up, axis, [(d, (d + 1) % ways) for d in range(ways)])]
    ppermute x16, waiting for transfers between devices: 61.6 us -> 55.4 us  [from_behind(): return lax.ppermute(block, axis, route)]
  transfers between devices with their start and end apart: 20 -> 34, of which waited for: 19 -> 24; matrix products, arithmetic and copies ran while one was open for 14% -> 19% of each run, Pallas kernels for 0% -> 0%
where the time goes in v1:
time: 456 us; the launch traced here: 454 us
  waiting for transfers between devices  136 us (30%)
  blocking collectives  101 us (22%)
  starting transfers between devices  87.7 us (19%)
  local copies, waits for them, and re-layouts  75.8 us (17%)
  matrix products  20 us (4%)
  other arithmetic  16.5 us (4%)
  between operations  14.3 us (3%)
    psum x1, blocking collectives, body(): mix_total, loss_total = lax.psum((mix_sum, kl_rows), ('seq', 'dp'))  101 us
    reduce_scatter x1, waiting for transfers between devices, body(): lax.psum_scatter((key_grad * factor)[None], 'head', scatter_dimension=2,...  60.8 us
    ppermute x16, waiting for transfers between devices, from_behind(): return lax.ppermute(block, axis, route)  55.4 us
    ppermute x7, starting transfers between devices, collect(): lax.ppermute(going_down, axis, [(d, (d - 1) % ways) for d in range(ways)])  36.4 us
    ppermute x16, starting transfers between devices, from_behind(): return lax.ppermute(block, axis, route)  33.9 us
    ppermute x8, starting transfers between devices, collect(): lax.ppermute(going_up, axis, [(d, (d + 1) % ways) for d in range(ways)])  17.2 us
    reduce_sum x128, local copies, waits for them, and re-layouts, pair_terms(): mixed_rows.append(jnp.sum(head_mix[:, index, None, None] * excess, axis=0))  15.2 us
    dynamic_slice x15, local copies, waits for them, and re-layouts, second_pass(): key_s = lax.dynamic_slice_in_dim(keys_s, start, row_count, 0)  13.8 us
  transfers between devices with their start and end apart: 34, of which 24 were waited for; matrix products, arithmetic and copies ran while one was open for 19% of the time, Pallas kernels for 0%

profile of v1, /device:TPU:32, one launch (start us, length us, event | category | flops | bytes accessed | tf_op | source)
XLA Modules:
  0.0 454.3 jit_solution(8675046888580790079)
XLA Ops:
  8.2 3.8 collective-permute-start.1
  12.1 5.5 %collective-permute-start.2 = (bf16[1,128,512]{1,2,0:T(8,128)(2,1)S(1)}, bf16[1,128,512]{1,2,0:T(8,128)(2,1)S(1)}, u32[]{:S(2)}, u32[]{:S(2)}) collective-permute-start(bf16[1,128,512]{1,2,0:T(8,128)(2,1)S(1)} %copy.156), channel_id=1, source_target_pairs={{0,60},{4,0},{8,4},{12,8},{16,12},{20,16},{24,20},{28,24},{32,28},... | collective-permute-start | bytes 393224 | tf_op jit(solution)/shard_map/ppermute | solution.py:24
  24.3 1.9 collective-permute-start.3
  26.3 6.0 %collective-permute-start.4 = (bf16[1,128,512]{1,2,0:T(8,128)(2,1)S(1)}, bf16[1,128,512]{1,2,0:T(8,128)(2,1)S(1)}, u32[]{:S(2)}, u32[]{:S(2)}) collective-permute-start(bf16[1,128,512]{1,2,0:T(8,128)(2,1)S(1)} %collective-permute-done.2), channel_id=1, source_target_pairs={{0,60},{4,0},{8,4},{12,8},{16,12},{20,16},{24,20},{28,24},{32,28},... | collective-permute-start | bytes 393224 | tf_op jit(solution)/shard_map/ppermute | solution.py:24
  33.7 1.9 collective-permute-start.5
  35.6 5.2 %collective-permute-start.6 = (bf16[1,128,512]{1,2,0:T(8,128)(2,1)S(1)}, bf16[1,128,512]{1,2,0:T(8,128)(2,1)S(1)}, u32[]{:S(2)}, u32[]{:S(2)}) collective-permute-start(bf16[1,128,512]{1,2,0:T(8,128)(2,1)S(1)} %collective-permute-done.4), channel_id=1, source_target_pairs={{0,60},{4,0},{8,4},{12,8},{16,12},{20,16},{24,20},{28,24},{32,28},... | collective-permute-start | bytes 393224 | tf_op jit(solution)/shard_map/ppermute | solution.py:24
  42.2 1.9 collective-permute-start.7
  44.1 5.2 %collective-permute-start.8 = (bf16[1,128,512]{1,2,0:T(8,128)(2,1)S(1)}, bf16[1,128,512]{1,2,0:T(8,128)(2,1)S(1)}, u32[]{:S(2)}, u32[]{:S(2)}) collective-permute-start(bf16[1,128,512]{1,2,0:T(8,128)(2,1)S(1)} %collective-permute-done.6), channel_id=1, source_target_pairs={{0,60},{4,0},{8,4},{12,8},{16,12},{20,16},{24,20},{28,24},{32,28},... | collective-permute-start | bytes 393224 | tf_op jit(solution)/shard_map/ppermute | solution.py:24
  51.5 1.9 collective-permute-start.9
  53.4 4.6 %collective-permute-start.10 = (bf16[1,128,512]{1,2,0:T(8,128)(2,1)S(1)}, bf16[1,128,512]{1,2,0:T(8,128)(2,1)S(1)}, u32[]{:S(2)}, u32[]{:S(2)}) collective-permute-start(bf16[1,128,512]{1,2,0:T(8,128)(2,1)S(1)} %collective-permute-done.8), channel_id=1, source_target_pairs={{0,60},{4,0},{8,4},{12,8},{16,12},{20,16},{24,20},{28,24},{32,28},... | collective-permute-start | bytes 393224 | tf_op jit(solution)/shard_map/ppermute | solution.py:24
  60.1 1.9 collective-permute-start.11
  62.0 4.8 %collective-permute-start.12 = (bf16[1,128,512]{1,2,0:T(8,128)(2,1)S(1)}, bf16[1,128,512]{1,2,0:T(8,128)(2,1)S(1)}, u32[]{:S(2)}, u32[]{:S(2)}) collective-permute-start(bf16[1,128,512]{1,2,0:T(8,128)(2,1)S(1)} %collective-permute-done.10), channel_id=1, source_target_pairs={{0,60},{4,0},{8,4},{12,8},{16,12},{20,16},{24,20},{28,24},{32,28},... | collective-permute-start | bytes 393224 | tf_op jit(solution)/shard_map/ppermute | solution.py:24
  70.3 5.2 %collective-permute-start.14 = (bf16[1,128,512]{1,2,0:T(8,128)(2,1)S(1)}, bf16[1,128,512]{1,2,0:T(8,128)(2,1)S(1)}, u32[]{:S(2)}, u32[]{:S(2)}) collective-permute-start(bf16[1,128,512]{1,2,0:T(8,128)(2,1)S(1)} %collective-permute-done.12), channel_id=1, source_target_pairs={{0,60},{4,0},{8,4},{12,8},{16,12},{20,16},{24,20},{28,24},{32,28},... | collective-permute-start | bytes 393224 | tf_op jit(solution)/shard_map/ppermute | solution.py:24
  80.2 5.4 %collective-permute-done.15 = bf16[1,128,512]{1,2,0:T(8,128)(2,1)S(1)} collective-permute-done((bf16[1,128,512]{1,2,0:T(8,128)(2,1)S(1)}, bf16[1,128,512]{1,2,0:T(8,128)(2,1)S(1)}, u32[]{:S(2)}, u32[]{:S(2)}) %collective-permute-start.15) | collective-permute-done | bytes 131104 | tf_op jit(solution)/shard_map/ppermute | solution.py:21
  86.3 12.6 %all-gather.2.cloned.1.call-done = bf16[1,2048,384]{1,2,0:T(8,128)(2,1)} async-done(((bf16[1,128,384]{1,2,0:T(8,128)(2,1)}), bf16[1,2048,384]{1,2,0:T(8,128)(2,1)}) %all-gather.2.cloned.1.call-update) | async-done | bytes 1572880 | tf_op jit(solution)/shard_map/all_gather | solution.py:128
  98.9 22.7 %while.42 = (s32[]{:T(128)}, f32[3,128]{1,0:T(4,128)S(1)}, f32[3,128]{1,0:T(4,128)S(1)}, f32[3,128]{1,0:T(4,128)S(1)}, f32[3,128]{1,0:T(4,128)S(1)}, /*index=5*/...) while((s32[]{:T(128)}, f32[3,128]{1,0:T(4,128)S(1)}, ...), condition=%wide.region_5.6_spmd.clone, body=%wide.region_0.5_spmd.clone.sunk | while | flops 125243136 | bytes 19275332 | solution.py:143
  124.0 150.1 %while.41 = (s32[]{:T(128)}, f32[3,128]{1,0:T(4,128)S(1)}, f32[3,8]{0,1:T(8,128)S(1)}, f32[128,512]{0,1:T(8,128)S(1)}, f32[128,512]{0,1:T(8,128)S(1)}, /*index=5...) while((s32[]{:T(128)}, f32[3,128]{1,0:T(4,128)S(1)}, ...), condition=%wide.region_41.42_spmd, body=%wide.region_23.41_spmd.sunk | while | flops 66486288 | bytes 9580356 | solution.py:168
  124.0 2.9 collective-permute-start
  132.3 2.9 collective-permute-start
  140.6 2.9 collective-permute-start
  150.0 2.0 collective-permute-start
  156.7 3.7 collective-permute-done
  160.4 1.9 collective-permute-start
  166.9 5.2 %collective-permute-done = f32[128,512]{0,1:T(8,128)S(1)} collective-permute-done((f32[128,512]{0,1:T(8,128)S(1)}, f32[128,512]{0,1:T(8,128)S(1)}, u32[]{:S(2)}, u32[]{:S(2)}) %collective-permute-start) | collective-permute-done | bytes 262176 | tf_op jit(solution)/shard_map/while/body/eval_jaxpr/ppermute | solution.py:34
  172.2 1.9 collective-permute-start
  178.7 5.7 %collective-permute-done = f32[128,512]{0,1:T(8,128)S(1)} collective-permute-done((f32[128,512]{0,1:T(8,128)S(1)}, f32[128,512]{0,1:T(8,128)S(1)}, u32[]{:S(2)}, u32[]{:S(2)}) %collective-permute-start) | collective-permute-done | bytes 262176 | tf_op jit(solution)/shard_map/while/body/eval_jaxpr/ppermute | solution.py:34
  184.4 1.9 collective-permute-start
  191.0 4.3 collective-permute-done
  195.3 1.9 collective-permute-start
  201.9 3.4 collective-permute-done
  205.3 1.9 collective-permute-start
  211.9 2.6 collective-permute-done
  214.6 1.9 collective-permute-start
  221.1 2.9 collective-permute-done
  224.1 1.9 collective-permute-start
  230.6 2.9 collective-permute-done
  233.6 2.0 collective-permute-start
  240.2 3.6 collective-permute-done
  243.9 1.9 collective-permute-start
  250.5 4.3 collective-permute-done
  254.8 1.9 collective-permute-start
  261.4 3.2 collective-permute-done
  264.6 1.9 collective-permute-start
  271.2 2.9 collective-permute-done
  274.9 1.9 collective-permute-start.16
  276.9 7.5 %collective-permute-done.16 = f32[128,512]{0,1:T(8,128)S(1)} collective-permute-done((f32[128,512]{0,1:T(8,128)S(1)}, f32[128,512]{0,1:T(8,128)S(1)}, u32[]{:S(2)}, u32[]{:S(2)}) %collective-permute-start.16) | collective-permute-done | bytes 262176 | tf_op jit(solution)/shard_map/ppermute | solution.py:34
  285.3 100.6 %all-reduce = (f32[3,8]{1,0:T(4,128)S(1)}, f32[3]{0:T(128)S(1)}) all-reduce(f32[3,8]{1,0:T(4,128)S(1)} %copy.183, f32[3]{0:T(128)S(1)} %add_reduce_fusion), channel_id=1, replica_groups=mesh['head'=8,'seq'=16,'dp'=4] {'seq','dp'}, use_global_device_ids=true, to_apply=%region_44.45 | all-reduce | flops 27 | bytes 216 | tf_op jit(solution)/shard_map/psum | solution.py:181
  387.0 60.8 %reduce-scatter.5.cloned.1.call-done = f32[1,128,64]{1,2,0:T(8,128)} async-done(((f32[1,128,512]{1,2,0:T(8,128)}), f32[1,128,64]{1,2,0:T(8,128)}) %reduce-scatter.5.cloned.1.call-update) | async-done | bytes 32784 | tf_op jit(solution)/shard_map/reduce_scatter | solution.py:178
  (635 shorter events, 121.3 us)
Async XLA Ops:
  7.2 91.7 %all-gather.2.cloned.1.call-start = ((), (), s32[]{:S(2)}) async-start(), calls=%async_computation.2 | async-start | bytes 1671168 | tf_op jit(solution)/shard_map/all_gather | solution.py:128
  8.2 16.1 %collective-permute-start.1 = (bf16[1,128,512]{1,2,0:T(8,128)(2,1)S(1)}, bf16[1,128,512]{1,2,0:T(8,128)(2,1)S(1)}, u32[]{:S(2)}, u32[]{:S(2)}) collective-permute-start(bf16[1,128,512]{1,2,0:T(8,128)(2,1)S(1)} %copy.156), channel_id=1, source_target_pairs={{0,4},{4,8},{8,12},{12,16},{16,20},{20,24},{24,28},{28,32},{32,36}... | collective-permute-start | bytes 393224 | tf_op jit(solution)/shard_map/ppermute | solution.py:21
  12.1 14.2 %collective-permute-start.2 = (bf16[1,128,512]{1,2,0:T(8,128)(2,1)S(1)}, bf16[1,128,512]{1,2,0:T(8,128)(2,1)S(1)}, u32[]{:S(2)}, u32[]{:S(2)}) collective-permute-start(bf16[1,128,512]{1,2,0:T(8,128)(2,1)S(1)} %copy.156), channel_id=1, source_target_pairs={{0,60},{4,0},{8,4},{12,8},{16,12},{20,16},{24,20},{28,24},{32,28},... | collective-permute-start | bytes 393224 | tf_op jit(solution)/shard_map/ppermute | solution.py:24
  19.2 367.8 %reduce-scatter.3.cloned.1.call-start = ((), (), s32[]{:S(2)}) async-start(), calls=%async_computation.3 | async-start | bytes 294912 | tf_op jit(solution)/shard_map/reduce_scatter | solution.py:177
  20.6 2.4 copy-start.2
  20.6 2.5 copy-start.1
  24.3 9.3 %collective-permute-start.3 = (bf16[1,128,512]{1,2,0:T(8,128)(2,1)S(1)}, bf16[1,128,512]{1,2,0:T(8,128)(2,1)S(1)}, u32[]{:S(2)}, u32[]{:S(2)}) collective-permute-start(bf16[1,128,512]{1,2,0:T(8,128)(2,1)S(1)} %collective-permute-done.1), channel_id=1, source_target_pairs={{0,4},{4,8},{8,12},{12,16},{16,20},{20,24},{24,28},{28,32},{32,36}... | collective-permute-start | bytes 393224 | tf_op jit(solution)/shard_map/ppermute | solution.py:21
  26.3 9.3 %collective-permute-start.4 = (bf16[1,128,512]{1,2,0:T(8,128)(2,1)S(1)}, bf16[1,128,512]{1,2,0:T(8,128)(2,1)S(1)}, u32[]{:S(2)}, u32[]{:S(2)}) collective-permute-start(bf16[1,128,512]{1,2,0:T(8,128)(2,1)S(1)} %collective-permute-done.2), channel_id=1, source_target_pairs={{0,60},{4,0},{8,4},{12,8},{16,12},{20,16},{24,20},{28,24},{32,28},... | collective-permute-start | bytes 393224 | tf_op jit(solution)/shard_map/ppermute | solution.py:24
  33.7 8.5 %collective-permute-start.5 = (bf16[1,128,512]{1,2,0:T(8,128)(2,1)S(1)}, bf16[1,128,512]{1,2,0:T(8,128)(2,1)S(1)}, u32[]{:S(2)}, u32[]{:S(2)}) collective-permute-start(bf16[1,128,512]{1,2,0:T(8,128)(2,1)S(1)} %collective-permute-done.3), channel_id=1, source_target_pairs={{0,4},{4,8},{8,12},{12,16},{16,20},{20,24},{24,28},{28,32},{32,36}... | collective-permute-start | bytes 393224 | tf_op jit(solution)/shard_map/ppermute | solution.py:21
  35.6 8.5 %collective-permute-start.6 = (bf16[1,128,512]{1,2,0:T(8,128)(2,1)S(1)}, bf16[1,128,512]{1,2,0:T(8,128)(2,1)S(1)}, u32[]{:S(2)}, u32[]{:S(2)}) collective-permute-start(bf16[1,128,512]{1,2,0:T(8,128)(2,1)S(1)} %collective-permute-done.4), channel_id=1, source_target_pairs={{0,60},{4,0},{8,4},{12,8},{16,12},{20,16},{24,20},{28,24},{32,28},... | collective-permute-start | bytes 393224 | tf_op jit(solution)/shard_map/ppermute | solution.py:24
  42.2 9.3 %collective-permute-start.7 = (bf16[1,128,512]{1,2,0:T(8,128)(2,1)S(1)}, bf16[1,128,512]{1,2,0:T(8,128)(2,1)S(1)}, u32[]{:S(2)}, u32[]{:S(2)}) collective-permute-start(bf16[1,128,512]{1,2,0:T(8,128)(2,1)S(1)} %collective-permute-done.5), channel_id=1, source_target_pairs={{0,4},{4,8},{8,12},{12,16},{16,20},{20,24},{24,28},{28,32},{32,36}... | collective-permute-start | bytes 393224 | tf_op jit(solution)/shard_map/ppermute | solution.py:21
  44.1 9.3 %collective-permute-start.8 = (bf16[1,128,512]{1,2,0:T(8,128)(2,1)S(1)}, bf16[1,128,512]{1,2,0:T(8,128)(2,1)S(1)}, u32[]{:S(2)}, u32[]{:S(2)}) collective-permute-start(bf16[1,128,512]{1,2,0:T(8,128)(2,1)S(1)} %collective-permute-done.6), channel_id=1, source_target_pairs={{0,60},{4,0},{8,4},{12,8},{16,12},{20,16},{24,20},{28,24},{32,28},... | collective-permute-start | bytes 393224 | tf_op jit(solution)/shard_map/ppermute | solution.py:24
  51.5 8.6 %collective-permute-start.9 = (bf16[1,128,512]{1,2,0:T(8,128)(2,1)S(1)}, bf16[1,128,512]{1,2,0:T(8,128)(2,1)S(1)}, u32[]{:S(2)}, u32[]{:S(2)}) collective-permute-start(bf16[1,128,512]{1,2,0:T(8,128)(2,1)S(1)} %collective-permute-done.7), channel_id=1, source_target_pairs={{0,4},{4,8},{8,12},{12,16},{16,20},{20,24},{24,28},{28,32},{32,36}... | collective-permute-start | bytes 393224 | tf_op jit(solution)/shard_map/ppermute | solution.py:21
  53.4 8.6 %collective-permute-start.10 = (bf16[1,128,512]{1,2,0:T(8,128)(2,1)S(1)}, bf16[1,128,512]{1,2,0:T(8,128)(2,1)S(1)}, u32[]{:S(2)}, u32[]{:S(2)}) collective-permute-start(bf16[1,128,512]{1,2,0:T(8,128)(2,1)S(1)} %collective-permute-done.8), channel_id=1, source_target_pairs={{0,60},{4,0},{8,4},{12,8},{16,12},{20,16},{24,20},{28,24},{32,28},... | collective-permute-start | bytes 393224 | tf_op jit(solution)/shard_map/ppermute | solution.py:24
  60.1 8.2 %collective-permute-start.11 = (bf16[1,128,512]{1,2,0:T(8,128)(2,1)S(1)}, bf16[1,128,512]{1,2,0:T(8,128)(2,1)S(1)}, u32[]{:S(2)}, u32[]{:S(2)}) collective-permute-start(bf16[1,128,512]{1,2,0:T(8,128)(2,1)S(1)} %collective-permute-done.9), channel_id=1, source_target_pairs={{0,4},{4,8},{8,12},{12,16},{16,20},{20,24},{24,28},{28,32},{32,36}... | collective-permute-start | bytes 393224 | tf_op jit(solution)/shard_map/ppermute | solution.py:21
  62.0 8.2 %collective-permute-start.12 = (bf16[1,128,512]{1,2,0:T(8,128)(2,1)S(1)}, bf16[1,128,512]{1,2,0:T(8,128)(2,1)S(1)}, u32[]{:S(2)}, u32[]{:S(2)}) collective-permute-start(bf16[1,128,512]{1,2,0:T(8,128)(2,1)S(1)} %collective-permute-done.10), channel_id=1, source_target_pairs={{0,60},{4,0},{8,4},{12,8},{16,12},{20,16},{24,20},{28,24},{32,28},... | collective-permute-start | bytes 393224 | tf_op jit(solution)/shard_map/ppermute | solution.py:24
  68.3 8.6 %collective-permute-start.13 = (bf16[1,128,512]{1,2,0:T(8,128)(2,1)S(1)}, bf16[1,128,512]{1,2,0:T(8,128)(2,1)S(1)}, u32[]{:S(2)}, u32[]{:S(2)}) collective-permute-start(bf16[1,128,512]{1,2,0:T(8,128)(2,1)S(1)} %collective-permute-done.11), channel_id=1, source_target_pairs={{0,4},{4,8},{8,12},{12,16},{16,20},{20,24},{24,28},{28,32},{32,36}... | collective-permute-start | bytes 393224 | tf_op jit(solution)/shard_map/ppermute | solution.py:21
  70.3 9.3 %collective-permute-start.14 = (bf16[1,128,512]{1,2,0:T(8,128)(2,1)S(1)}, bf16[1,128,512]{1,2,0:T(8,128)(2,1)S(1)}, u32[]{:S(2)}, u32[]{:S(2)}) collective-permute-start(bf16[1,128,512]{1,2,0:T(8,128)(2,1)S(1)} %collective-permute-done.12), channel_id=1, source_target_pairs={{0,60},{4,0},{8,4},{12,8},{16,12},{20,16},{24,20},{28,24},{32,28},... | collective-permute-start | bytes 393224 | tf_op jit(solution)/shard_map/ppermute | solution.py:24
  76.9 8.7 %collective-permute-start.15 = (bf16[1,128,512]{1,2,0:T(8,128)(2,1)S(1)}, bf16[1,128,512]{1,2,0:T(8,128)(2,1)S(1)}, u32[]{:S(2)}, u32[]{:S(2)}) collective-permute-start(bf16[1,128,512]{1,2,0:T(8,128)(2,1)S(1)} %collective-permute-done.13), channel_id=1, source_target_pairs={{0,4},{4,8},{8,12},{12,16},{16,20},{20,24},{24,28},{28,32},{32,36}... | collective-permute-start | bytes 393224 | tf_op jit(solution)/shard_map/ppermute | solution.py:21
  98.9 22.8 %copy-start = (bf16[1,128,384]{1,2,0:T(8,128)(2,1)S(1)}, bf16[1,128,384]{1,2,0:T(8,128)(2,1)}, u32[]{:S(2)}) copy-start(bf16[1,128,384]{1,2,0:T(8,128)(2,1)} %copy.152) | copy-start | bytes 294916
  124.0 8.3 %collective-permute-start = (f32[128,512]{0,1:T(8,128)S(1)}, f32[128,512]{0,1:T(8,128)S(1)}, u32[]{:S(2)}, u32[]{:S(2)}) collective-permute-start(f32[128,512]{0,1:T(8,128)S(1)} %get-tuple-element.1076), channel_id=1, source_target_pairs={{60,0},{0,4},{4,8},{8,12},{12,16},{16,20},{20,24},{24,28},{28,32},... | collective-permute-start | bytes 786440 | tf_op jit(solution)/shard_map/while/body/eval_jaxpr/ppermute | solution.py:34
  132.3 8.3 %collective-permute-start = (f32[128,512]{0,1:T(8,128)S(1)}, f32[128,512]{0,1:T(8,128)S(1)}, u32[]{:S(2)}, u32[]{:S(2)}) collective-permute-start(f32[128,512]{0,1:T(8,128)S(1)} %get-tuple-element.1076), channel_id=1, source_target_pairs={{60,0},{0,4},{4,8},{8,12},{12,16},{16,20},{20,24},{24,28},{28,32},... | collective-permute-start | bytes 786440 | tf_op jit(solution)/shard_map/while/body/eval_jaxpr/ppermute | solution.py:34
  140.6 9.3 %collective-permute-start = (f32[128,512]{0,1:T(8,128)S(1)}, f32[128,512]{0,1:T(8,128)S(1)}, u32[]{:S(2)}, u32[]{:S(2)}) collective-permute-start(f32[128,512]{0,1:T(8,128)S(1)} %get-tuple-element.1076), channel_id=1, source_target_pairs={{60,0},{0,4},{4,8},{8,12},{12,16},{16,20},{20,24},{24,28},{28,32},... | collective-permute-start | bytes 786440 | tf_op jit(solution)/shard_map/while/body/eval_jaxpr/ppermute | solution.py:34
  150.0 10.3 %collective-permute-start = (f32[128,512]{0,1:T(8,128)S(1)}, f32[128,512]{0,1:T(8,128)S(1)}, u32[]{:S(2)}, u32[]{:S(2)}) collective-permute-start(f32[128,512]{0,1:T(8,128)S(1)} %get-tuple-element.1076), channel_id=1, source_target_pairs={{60,0},{0,4},{4,8},{8,12},{12,16},{16,20},{20,24},{24,28},{28,32},... | collective-permute-start | bytes 786440 | tf_op jit(solution)/shard_map/while/body/eval_jaxpr/ppermute | solution.py:34
  160.4 11.7 %collective-permute-start = (f32[128,512]{0,1:T(8,128)S(1)}, f32[128,512]{0,1:T(8,128)S(1)}, u32[]{:S(2)}, u32[]{:S(2)}) collective-permute-start(f32[128,512]{0,1:T(8,128)S(1)} %get-tuple-element.1076), channel_id=1, source_target_pairs={{60,0},{0,4},{4,8},{8,12},{12,16},{16,20},{20,24},{24,28},{28,32},... | collective-permute-start | bytes 786440 | tf_op jit(solution)/shard_map/while/body/eval_jaxpr/ppermute | solution.py:34
  172.2 12.2 %collective-permute-start = (f32[128,512]{0,1:T(8,128)S(1)}, f32[128,512]{0,1:T(8,128)S(1)}, u32[]{:S(2)}, u32[]{:S(2)}) collective-permute-start(f32[128,512]{0,1:T(8,128)S(1)} %get-tuple-element.1076), channel_id=1, source_target_pairs={{60,0},{0,4},{4,8},{8,12},{12,16},{16,20},{20,24},{24,28},{28,32},... | collective-permute-start | bytes 786440 | tf_op jit(solution)/shard_map/while/body/eval_jaxpr/ppermute | solution.py:34
  184.4 10.8 %collective-permute-start = (f32[128,512]{0,1:T(8,128)S(1)}, f32[128,512]{0,1:T(8,128)S(1)}, u32[]{:S(2)}, u32[]{:S(2)}) collective-permute-start(f32[128,512]{0,1:T(8,128)S(1)} %get-tuple-element.1076), channel_id=1, source_target_pairs={{60,0},{0,4},{4,8},{8,12},{12,16},{16,20},{20,24},{24,28},{28,32},... | collective-permute-start | bytes 786440 | tf_op jit(solution)/shard_map/while/body/eval_jaxpr/ppermute | solution.py:34
  195.3 10.0 %collective-permute-start = (f32[128,512]{0,1:T(8,128)S(1)}, f32[128,512]{0,1:T(8,128)S(1)}, u32[]{:S(2)}, u32[]{:S(2)}) collective-permute-start(f32[128,512]{0,1:T(8,128)S(1)} %get-tuple-element.1076), channel_id=1, source_target_pairs={{60,0},{0,4},{4,8},{8,12},{12,16},{16,20},{20,24},{24,28},{28,32},... | collective-permute-start | bytes 786440 | tf_op jit(solution)/shard_map/while/body/eval_jaxpr/ppermute | solution.py:34
  205.3 9.2 %collective-permute-start = (f32[128,512]{0,1:T(8,128)S(1)}, f32[128,512]{0,1:T(8,128)S(1)}, u32[]{:S(2)}, u32[]{:S(2)}) collective-permute-start(f32[128,512]{0,1:T(8,128)S(1)} %get-tuple-element.1076), channel_id=1, source_target_pairs={{60,0},{0,4},{4,8},{8,12},{12,16},{16,20},{20,24},{24,28},{28,32},... | collective-permute-start | bytes 786440 | tf_op jit(solution)/shard_map/while/body/eval_jaxpr/ppermute | solution.py:34
  214.6 9.5 %collective-permute-start = (f32[128,512]{0,1:T(8,128)S(1)}, f32[128,512]{0,1:T(8,128)S(1)}, u32[]{:S(2)}, u32[]{:S(2)}) collective-permute-start(f32[128,512]{0,1:T(8,128)S(1)} %get-tuple-element.1076), channel_id=1, source_target_pairs={{60,0},{0,4},{4,8},{8,12},{12,16},{16,20},{20,24},{24,28},{28,32},... | collective-permute-start | bytes 786440 | tf_op jit(solution)/shard_map/while/body/eval_jaxpr/ppermute | solution.py:34
  224.1 9.5 %collective-permute-start = (f32[128,512]{0,1:T(8,128)S(1)}, f32[128,512]{0,1:T(8,128)S(1)}, u32[]{:S(2)}, u32[]{:S(2)}) collective-permute-start(f32[128,512]{0,1:T(8,128)S(1)} %get-tuple-element.1076), channel_id=1, source_target_pairs={{60,0},{0,4},{4,8},{8,12},{12,16},{16,20},{20,24},{24,28},{28,32},... | collective-permute-start | bytes 786440 | tf_op jit(solution)/shard_map/while/body/eval_jaxpr/ppermute | solution.py:34
  233.6 10.2 %collective-permute-start = (f32[128,512]{0,1:T(8,128)S(1)}, f32[128,512]{0,1:T(8,128)S(1)}, u32[]{:S(2)}, u32[]{:S(2)}) collective-permute-start(f32[128,512]{0,1:T(8,128)S(1)} %get-tuple-element.1076), channel_id=1, source_target_pairs={{60,0},{0,4},{4,8},{8,12},{12,16},{16,20},{20,24},{24,28},{28,32},... | collective-permute-start | bytes 786440 | tf_op jit(solution)/shard_map/while/body/eval_jaxpr/ppermute | solution.py:34
  243.9 10.9 %collective-permute-start = (f32[128,512]{0,1:T(8,128)S(1)}, f32[128,512]{0,1:T(8,128)S(1)}, u32[]{:S(2)}, u32[]{:S(2)}) collective-permute-start(f32[128,512]{0,1:T(8,128)S(1)} %get-tuple-element.1076), channel_id=1, source_target_pairs={{60,0},{0,4},{4,8},{8,12},{12,16},{16,20},{20,24},{24,28},{28,32},... | collective-permute-start | bytes 786440 | tf_op jit(solution)/shard_map/while/body/eval_jaxpr/ppermute | solution.py:34
  254.8 9.8 %collective-permute-start = (f32[128,512]{0,1:T(8,128)S(1)}, f32[128,512]{0,1:T(8,128)S(1)}, u32[]{:S(2)}, u32[]{:S(2)}) collective-permute-start(f32[128,512]{0,1:T(8,128)S(1)} %get-tuple-element.1076), channel_id=1, source_target_pairs={{60,0},{0,4},{4,8},{8,12},{12,16},{16,20},{20,24},{24,28},{28,32},... | collective-permute-start | bytes 786440 | tf_op jit(solution)/shard_map/while/body/eval_jaxpr/ppermute | solution.py:34
  264.6 9.5 %collective-permute-start = (f32[128,512]{0,1:T(8,128)S(1)}, f32[128,512]{0,1:T(8,128)S(1)}, u32[]{:S(2)}, u32[]{:S(2)}) collective-permute-start(f32[128,512]{0,1:T(8,128)S(1)} %get-tuple-element.1076), channel_id=1, source_target_pairs={{60,0},{0,4},{4,8},{8,12},{12,16},{16,20},{20,24},{24,28},{28,32},... | collective-permute-start | bytes 786440 | tf_op jit(solution)/shard_map/while/body/eval_jaxpr/ppermute | solution.py:34
  274.9 172.9 %reduce-scatter.5.cloned.1.call-start = ((), (), s32[]{:S(2)}) async-start(), calls=%async_computation.4 | async-start | bytes 294912 | tf_op jit(solution)/shard_map/reduce_scatter | solution.py:178
  274.9 9.5 %collective-permute-start.16 = (f32[128,512]{0,1:T(8,128)S(1)}, f32[128,512]{0,1:T(8,128)S(1)}, u32[]{:S(2)}, u32[]{:S(2)}) collective-permute-start(f32[128,512]{0,1:T(8,128)S(1)} %get-tuple-element.493), channel_id=1, source_target_pairs={{60,0},{0,4},{4,8},{8,12},{12,16},{16,20},{20,24},{24,28},{28,32},... | collective-permute-start | bytes 786440 | tf_op jit(solution)/shard_map/ppermute | solution.py:34
Sparse Core Ops, SparseCore 0:
  19.3 79.5 all-gather.1
  275.0 82.6 reduce-scatter.2
  362.6 85.1 reduce-scatter.4
